TPU v7x, 32 devices: a whole 2x2x4 slice. The times are simulated.
32 devices in a mesh: seq: 4 (over y, x), res: 8 (over z, core).
Axes of the slice: x: 2, y: 2, z: 4, core: 2. Of those that a mesh axis runs over, the one named last changes fastest.
Arguments:
- alignment: float32 [256, 64, 256], P('seq', 'res'), may hold values from -100 to 100
- pair_features: float32 [64, 64, 128], P('seq', 'res'), may hold values from -100 to 100
- outer_gain: float32 [256], replicated, may hold values from 0.5 to 1.5
- w_outer_in: float32 [256, 64], replicated, may hold values from -0.375 to 0.375
- w_outer_out: float32 [1024, 128], replicated, may hold values from -0.1875 to 0.1875
- pair_gain: float32 [128], replicated, may hold values from 0.5 to 1.5
- w_bias: float32 [128, 8], replicated, may hold values from -30 to 30
- row_gain: float32 [256], replicated, may hold values from 0.5 to 1.5
- w_project: float32 [256, 1024], replicated, may hold values from -0.375 to 0.375
- w_output: float32 [256, 256], replicated, may hold values from -0.375 to 0.375
Outputs:
- alignment_out: float32 [256, 64, 256], P('seq', 'res')
- updated_pair_array: float32 [64, 64, 128], P('seq', 'res')
All inputs are finite; a program needn't handle non-finite values.
Results may differ from a plain program's by a relative error of at most 0.00018.
Values sent between devices are 32-bit elements; how exact they have to be, the bound alone decides.
A program may use at most 128 MiB of HBM per device.

v0:
```python
import jax
import jax.numpy as jnp
from jax import lax
from jax.sharding import PartitionSpec as P

precise = lax.Precision.HIGHEST


def layer_norm(values, scales):
    average = jnp.mean(values, axis=-1, keepdims=True)
    centered = values - average
    variance = jnp.mean(centered * centered, axis=-1, keepdims=True)
    return centered * lax.rsqrt(variance + 1e-05) * scales


def row_attention(sequence, bias_all, row_gain, w_project, w_output):
    residues, channels = sequence.shape
    head_count = bias_all.shape[0]
    head_size = channels // head_count
    normed_rows = layer_norm(sequence, row_gain)
    projected = jnp.dot(
        normed_rows, w_project, precision=precise, preferred_element_type=jnp.float32
    )
    query_map = projected[:, :channels].reshape(residues, head_count, head_size) * head_size ** (
        -0.5
    )
    key_map = projected[:, channels : 2 * channels].reshape(residues, head_count, head_size)
    value_map = projected[:, 2 * channels : 3 * channels].reshape(residues, head_count, head_size)
    gate_map = projected[:, 3 * channels :]
    scores = jnp.einsum("ihd,jhd->hij", query_map, key_map, precision=precise) + bias_all
    weights = jax.nn.softmax(scores, axis=-1)
    mixed_heads = jnp.einsum("hij,jhd->ihd", weights, value_map, precision=precise).reshape(
        residues, channels
    )
    gated_out = jax.nn.sigmoid(gate_map) * mixed_heads
    return sequence + jnp.dot(
        gated_out, w_output, precision=precise, preferred_element_type=jnp.float32
    )


def on_device(
    alignment,
    pair_features,
    outer_gain,
    w_outer_in,
    w_outer_out,
    pair_gain,
    w_bias,
    row_gain,
    w_project,
    w_output,
):
    sequence_local_count, residue_local_count, alignment_channel_count = alignment.shape
    row_block = pair_features.shape[0]
    sequence_group_list = lax.axis_size("res")
    seq_groups = lax.axis_size("seq")
    seq_total = sequence_local_count * seq_groups
    channels = w_outer_in.shape[1] // 2
    normed_rows = layer_norm(alignment, outer_gain)
    both_maps = jnp.einsum("src,cd->sdr", normed_rows, w_outer_in, precision=precise)
    left_maps = both_maps[:, :channels]
    right_maps = both_maps[:, channels:]
    left_all = lax.all_gather(left_maps, "res", axis=2, tiled=True)
    left_rows = lax.all_to_all(left_all, "seq", split_axis=2, concat_axis=0, tiled=True)
    product = jnp.einsum(
        "sxi,syj->ijxy",
        left_rows,
        lax.all_gather(right_maps, "seq", axis=0, tiled=True),
        precision=precise,
    )
    summed = product.reshape(row_block, residue_local_count, channels * channels)
    pair_update = jnp.einsum("ijk,kc->ijc", summed / seq_total, w_outer_out, precision=precise)
    updated_pair_array = pair_features + pair_update
    bias_tile = jnp.einsum(
        "ijc,ch->hij", layer_norm(updated_pair_array, pair_gain), w_bias, precision=precise
    )
    bias_rows = lax.all_gather(bias_tile, "res", axis=2, tiled=True)
    bias_all = lax.all_gather(bias_rows, "seq", axis=1, tiled=True)
    sequence_grouped_rows = alignment.reshape(
        sequence_group_list,
        sequence_local_count // sequence_group_list,
        residue_local_count,
        alignment_channel_count,
    )
    sequences = lax.all_to_all(
        sequence_grouped_rows, "res", split_axis=0, concat_axis=2, tiled=True
    )[0]
    updated = jax.vmap(row_attention, in_axes=(0, None, None, None, None))(
        sequences, bias_all, row_gain, w_project, w_output
    )
    attended = updated[None]
    returned_result = lax.all_to_all(attended, "res", split_axis=2, concat_axis=0, tiled=True)
    return (
        returned_result.reshape(sequence_local_count, residue_local_count, alignment_channel_count),
        updated_pair_array,
    )


def solution(mesh):
    in_specs = (
        P("seq", "res", None),
        P("seq", "res", None),
        P(),
        P(),
        P(),
        P(),
        P(),
        P(),
        P(),
        P(),
    )
    out_specs = (P("seq", "res", None), P("seq", "res", None))
    return jax.shard_map(
        on_device, mesh=mesh, in_specs=in_specs, out_specs=out_specs, check_vma=False
    )
```

profile of v0, /device:TPU:0, one launch (start us, length us, event | category | flops | bytes accessed | tf_op | source)
XLA Modules:
  0.0 148.9 jit_solution(3641051938862273192)
XLA Ops:
  0.6 0.0 copy-start
  0.6 1.3 reduce_sum.65
  1.9 1.3 multiply_reduce_fusion
  3.2 1.7 %convolution_bitcast_fusion = f32[64,64,8]{1,2,0:T(8,128)S(1)} fusion(f32[64,8,256]{2,1,0:T(8,128)} %param.10, f32[256]{0:T(256)} %param.12, f32[64,8]{1,0:T(8,128)S(1)} %add_rsqrt_fusion, f32[64,8]{1,0:T(8,128)S(1)} %broadcast_multiply_fusion, f32[256,64]{0,1:T(8,128)} %param.13), kind=kOutput, calls=%fused_computation.8 | convolution fusion | flops 101056512 | bytes 726016 | tf_op jit(solution)/shard_map/src,cd->sdr/dot_general | solution.py:60
  4.9 0.1 fusion.40
  5.1 25.1 %all_gather.13 = f32[64,32,64]{1,2,0:T(8,128)S(1)} all-gather(f32[64,32,8]{1,2,0:T(8,128)S(1)} %get-tuple-element.5), channel_id=1, replica_groups=mesh['seq'=4,'res'=8] {'res'}, dimensions={2}, use_global_device_ids=true | all-gather | bytes 589824 | tf_op jit(solution)/shard_map/all_gather | solution.py:63
  30.2 2.1 %copy.39 = f32[64,32,64]{0,1,2:T(8,128)} copy(f32[64,32,64]{1,2,0:T(8,128)S(1)} %all_gather.13) | data formatting | bytes 1048576 | tf_op jit(solution)/shard_map/all_gather | solution.py:63
  32.3 2.7 %reshape.99 = f32[4,1,32768]{2,1,0:T(1,128)} reshape(f32[64,32,64]{2,1,0:T(8,128)} %bitcast.73) | data formatting | bytes 1048576
  35.0 3.7 %all-to-all-start.1 = ((f32[4,1,32768]{2,1,0:T(1,128)}), f32[4,1,32768]{2,1,0:T(1,128)S(1)}, u32[]{:S(2)}, u32[]{:S(2)}) async-start(f32[4,1,32768]{2,1,0:T(1,128)} %reshape.99), calls=%async_computation.1 | async-start | bytes 1048576 | tf_op jit(solution)/shard_map/all_to_all | solution.py:64
  38.7 18.5 %all_gather.12 = f32[256,32,8]{1,2,0:T(8,128)S(1)} all-gather(f32[64,32,8]{1,2,0:T(8,128)S(1)} %get-tuple-element.6), channel_id=1, replica_groups=mesh['seq'=4,'res'=8] {'seq'}, dimensions={0}, use_global_device_ids=true | all-gather | bytes 327680 | tf_op jit(solution)/shard_map/all_gather | solution.py:68
  57.2 0.4 copy.49
  57.6 4.3 %all-to-all-start = ((f32[8,8,8,256]{3,2,1,0:T(8,128)}), f32[8,8,8,256]{3,2,1,0:T(8,128)}, u32[]{:S(2)}, u32[]{:S(2)}) async-start(f32[8,8,8,256]{3,2,1,0:T(8,128)} %bitcast), calls=%async_computation | async-start | bytes 1048576 | tf_op jit(solution)/shard_map/all_to_all | solution.py:85
  62.0 0.5 broadcast.97
  62.5 2.1 %reduce.2 = f32[4,32768]{1,0:T(4,128)S(1)} reduce(f32[4,1,32768]{2,1,0:T(1,128)S(1)} %all-to-all-done.1, f32[]{:T(128)} %broadcast.97), dimensions={1}, to_apply=%all_to_all.38.reduce_sub_computation | reduce | bytes 1048580 | tf_op jit(solution)/shard_map/all_to_all | solution.py:64
  64.6 0.5 reshape.100
  65.2 0.7 copy.59
  65.9 0.6 reshape.94
  66.5 3.2 %multiply_bitcast_fusion = f32[16,8,32,32]{2,1,0,3:T(8,128)} fusion(f32[256,32,8,1]{0,2,3,1:T(8,128)S(1)} %copy.49, f32[256,32,16,1]{0,1,2,3:T(8,128)S(1)} %reshape.94), kind=kOutput, calls=%fused_computation.3 | convolution fusion | flops 402784256 | bytes 1310720 | tf_op jit(solution)/shard_map/sxi,syj->ijxy/dot_general | solution.py:65
  69.7 2.3 %copy.42 = f32[16,8,32,32]{3,2,1,0:T(8,128)S(1)} copy(f32[16,8,32,32]{2,1,0,3:T(8,128)} %multiply_bitcast_fusion) | data formatting | bytes 1048576 | tf_op jit(solution)/shard_map/div | solution.py:72
  71.9 0.0 copy-start.3
  71.9 0.0 copy-start.6
  72.0 1.7 %div.50 = f32[16,8,1024]{2,1,0:T(8,128)} reshape(f32[16,8,32,32]{3,2,1,0:T(8,128)S(1)} %copy.42) | data formatting | bytes 1048576 | tf_op jit(solution)/shard_map/div | solution.py:72
  73.7 1.9 %fusion.41 = (f32[16,8]{1,0:T(8,128)S(1)}, f32[16,8,128]{2,1,0:T(8,128)S(1)}) fusion(f32[16,8,128]{2,1,0:T(8,128)S(1)} %copy-done.3, f32[16,8,1024]{2,1,0:T(8,128)} %div.50, f32[1024,128]{1,0:T(8,128)} %param.14), kind=kOutput, calls=%fused_computation.60 | convolution fusion | flops 201359232 | bytes 1180160 | tf_op jit(solution)/shard_map/ijk,kc->ijc/dot_general | solution.py:72
  75.6 0.0 copy-start.2
  75.7 0.2 multiply_reduce_fusion.2
  75.8 0.3 convolution_bitcast_fusion.1
  76.1 14.9 %all_gather.14 = f32[8,16,64]{0,2,1:T(8,128)S(1)} all-gather(f32[8,16,8]{0,2,1:T(8,128)S(1)} %convolution_bitcast_fusion.1), channel_id=1, replica_groups=mesh['seq'=4,'res'=8] {'res'}, dimensions={2}, use_global_device_ids=true | all-gather | bytes 36864 | tf_op jit(solution)/shard_map/all_gather | solution.py:77
  91.1 0.2 copy.43
  91.2 8.4 %all_gather.15 = f32[8,64,64]{2,0,1:T(8,128)S(1)} all-gather(f32[8,16,64]{2,0,1:T(8,128)S(1)} %copy.43), channel_id=1, replica_groups=mesh['seq'=4,'res'=8] {'seq'}, dimensions={1}, use_global_device_ids=true | all-gather | bytes 163840 | tf_op jit(solution)/shard_map/all_gather | solution.py:78
  99.6 0.1 copy.44
  99.8 1.2 bitcast_reduce_fusion
  101.0 0.1 div.42
  101.1 1.3 multiply_reduce_fusion.1
  102.4 0.1 rsqrt.28
  102.5 2.9 %fusion.4 = f32[8,64,1024]{2,1,0:T(8,128)S(1)} fusion(f32[256,1024]{1,0:T(8,128)S(1)} %copy-done, f32[256]{0:T(256)S(1)} %copy-done.4, f32[8,64]{1,0:T(8,128)S(1)} %rsqrt.28, f32[8,64]{1,0:T(8,128)S(1)} %div.42, f32[8,8,8,256]{3,2,1,0:T(8,128)} %all-to-all-done), kind=kOutput, calls=%fused_computation.11 | convolution fusion | flops 1611005952 | bytes 3675136 | tf_op jit(solution)/shard_map/vmap()/dot_general | solution.py:21
  105.5 1.2 fusion.39
  106.7 2.4 %copy.38 = f32[8,64,256]{1,2,0:T(8,128)} copy(f32[8,64,256]{2,1,0:T(8,128)} %get-tuple-element.2) | data formatting | bytes 1048576 | tf_op jit(solution)/shard_map/vmap()/slice | solution.py:27
  109.1 2.4 %copy.37 = f32[8,64,256]{1,2,0:T(8,128)} copy(f32[8,64,256]{2,1,0:T(8,128)} %get-tuple-element.3) | data formatting | bytes 1048576 | tf_op jit(solution)/shard_map/vmap()/mul | solution.py:24
  111.5 2.4 %copy.36 = f32[8,64,256]{1,2,0:T(8,128)} copy(f32[8,64,256]{2,1,0:T(8,128)} %get-tuple-element.4) | data formatting | bytes 1048576 | tf_op jit(solution)/shard_map/vmap()/slice | solution.py:28
  113.8 5.1 %add_reduce_fusion = (f32[8,8,64]{2,1,0:T(8,128)S(1)}, f32[8,8,64,64]{2,3,1,0:T(8,128)S(1)}) fusion(f32[8,64,64]{1,2,0:T(8,128)S(1)} %copy.44, f32[8,64,8,32]{1,3,2,0:T(8,128)} %bitcast.72, f32[8,64,8,32]{1,3,2,0:T(8,128)} %bitcast.71), kind=kOutput, calls=%fused_computation.4 | convolution fusion | flops 101183488 | bytes 2244608 | tf_op jit(solution)/shard_map/vmap(ihd,jhd->hij)/dot_general | solution.py:30
  119.0 0.5 fusion.2
  119.5 0.7 copy-done.1
  120.2 3.3 %fusion = f32[8,8,32,64]{3,2,1,0:T(8,128)} fusion(f32[8,64,8,32]{1,3,2,0:T(8,128)S(1)} %bitcast.78, f32[8,8,64,64]{2,3,1,0:T(8,128)S(1)} %get-tuple-element.10, f32[8,8,64]{2,1,0:T(8,128)S(1)} %fusion.2, f32[8,8,64]{2,1,0:T(8,128)S(1)} %get-tuple-element.9, f32[8,64,64]{1,2,0:T(8,128)S(1)} %copy.44), kind=kOutput, calls=%fused_computation | convolution fusion | flops 101449728 | bytes 2260992 | tf_op jit(solution)/shard_map/vmap(hij,jhd->ihd)/dot_general | solution.py:32
  123.5 2.3 %copy.46 = f32[8,64,256]{2,1,0:T(8,128)} copy(f32[8,64,256]{1,2,0:T(8,128)} %bitcast.79) | data formatting | bytes 1048576 | tf_op jit(solution)/shard_map/vmap()/reshape | solution.py:32
  125.8 1.9 %fusion.3 = f32[1,8,64,256]{3,2,1,0:T(8,128)S(1)} fusion(f32[8,64,256]{2,1,0:T(8,128)} %copy.46, f32[8,64,1024]{2,1,0:T(8,128)S(1)} %fusion.4, f32[256,256]{1,0:T(8,128)} %param.19, f32[8,8,8,256]{3,2,1,0:T(8,128)} %all-to-all-done), kind=kOutput, calls=%fused_computation.7 | convolution fusion | flops 403308544 | bytes 2359296 | tf_op jit(solution)/shard_map/vmap()/dot_general | solution.py:36
  127.8 0.3 copy.47
  128.1 19.8 %all_to_all.48 = f32[1,8,64,256]{3,1,0,2:T(8,128)S(1)} all-to-all(f32[1,8,64,256]{3,1,0,2:T(8,128)S(1)} %copy.47), channel_id=1, replica_groups=mesh['seq'=4,'res'=8] {'res'}, dimensions={2} | all-to-all | bytes 1048576 | tf_op jit(solution)/shard_map/all_to_all | solution.py:92
  148.0 1.0 copy.48
  (19 shorter events, 0.1 us)
Async XLA Ops:
  0.6 101.9 %copy-start = (f32[256,1024]{1,0:T(8,128)S(1)}, f32[256,1024]{1,0:T(8,128)}, u32[]{:S(2)}) copy-start(f32[256,1024]{1,0:T(8,128)} %param.18) | copy-start | bytes 3145732
  35.0 22.6 %all-to-all-start.1 = ((f32[4,1,32768]{2,1,0:T(1,128)}), f32[4,1,32768]{2,1,0:T(1,128)S(1)}, u32[]{:S(2)}, u32[]{:S(2)}) async-start(f32[4,1,32768]{2,1,0:T(1,128)} %reshape.99), calls=%async_computation.1 | async-start | bytes 1048576 | tf_op jit(solution)/shard_map/all_to_all | solution.py:64
  57.6 42.2 %all-to-all-start = ((f32[8,8,8,256]{3,2,1,0:T(8,128)}), f32[8,8,8,256]{3,2,1,0:T(8,128)}, u32[]{:S(2)}, u32[]{:S(2)}) async-start(f32[8,8,8,256]{3,2,1,0:T(8,128)} %bitcast), calls=%async_computation | async-start | bytes 1048576 | tf_op jit(solution)/shard_map/all_to_all | solution.py:85
  71.9 1.8 %copy-start.3 = (f32[16,8,128]{2,1,0:T(8,128)S(1)}, f32[16,8,128]{2,1,0:T(8,128)}, u32[]{:S(2)}) copy-start(f32[16,8,128]{2,1,0:T(8,128)} %param.11) | copy-start | bytes 196612
  71.9 3.9 %copy-start.5 = (f32[128,8]{0,1:T(8,128)S(1)}, f32[128,8]{0,1:T(8,128)}, u32[]{:S(2)}) copy-start(f32[128,8]{0,1:T(8,128)} %param.16) | copy-start | bytes 12292
  71.9 3.9 %copy-start.6 = (f32[128]{0:T(128)S(1)}, f32[128]{0:T(128)}, u32[]{:S(2)}) copy-start(f32[128]{0:T(128)} %param.15) | copy-start | bytes 1540
  75.6 29.8 %copy-start.2 = (f32[16,8,128]{2,1,0:T(8,128)}, f32[16,8,128]{2,1,0:T(8,128)S(1)}, u32[]{:S(2)}) copy-start(f32[16,8,128]{2,1,0:T(8,128)S(1)} %get-tuple-element.8) | copy-start | bytes 196612
  75.6 26.9 %copy-start.4 = (f32[256]{0:T(256)S(1)}, f32[256]{0:T(256)}, u32[]{:S(2)}) copy-start(f32[256]{0:T(256)} %param.17) | copy-start | bytes 3076
  118.9 1.2 copy-start.1
where the time goes:
time: 150 us; the launch traced here: 149 us
  blocking collectives  86.8 us (58%)
  local copies, waits for them, and re-layouts  23.6 us (16%)
  matrix products  20.3 us (14%)
  other arithmetic  9.14 us (6%)
  starting transfers between devices  8.05 us (5%)
    all_gather x1, blocking collectives, on_device(): left_all = lax.all_gather(left_maps, 'res', axis=2, tiled=True)  25.1 us
    all_to_all x1, blocking collectives, on_device(): lax.all_to_all(attended, 'res', split_axis=2, concat_axis=0, tiled=True)  19.8 us
    all_gather x1, blocking collectives, on_device(): lax.all_gather(right_maps, 'seq', axis=0, tiled=True)  18.5 us
    all_gather x1, blocking collectives, on_device(): bias_rows = lax.all_gather(bias_tile, 'res', axis=2, tiled=True)  14.9 us
    all_gather x1, blocking collectives, on_device(): bias_all = lax.all_gather(bias_rows, 'seq', axis=1, tiled=True)  8.4 us
    dot_general x1, matrix products, row_attention(): jnp.einsum('ihd,jhd->hij', query_map, key_map, precision=precise) + bias_all  5.09 us
    all_to_all x1, starting transfers between devices, on_device(): lax.all_to_all(sequence_grouped_rows, 'res', split_axis=0, concat_axis=2,...  4.34 us
    div x2, local copies, waits for them, and re-layouts, on_device(): summed / seq_total  4 us
  transfers between devices with their start and end apart: 2, of which 0 were waited for; matrix products, arithmetic and copies ran while one was open for 10% of the time, Pallas kernels for 0%

commit v1 on v0

v1 whole, which is shorter than its diff:
```python
import functools
import jax
import jax.numpy as jnp
from jax import lax
from jax.experimental import pallas as pl
from jax.experimental.pallas import tpu as pltpu
from jax.sharding import PartitionSpec as P

F32 = jnp.float32
BF16 = jnp.bfloat16
MESH = pl.DeviceIdType.MESH
ROWS_COLS = (((1,), (0,)), ((), ()))
ROWS_ROWS = (((1,), (1,)), ((), ()))
COLS_COLS = (((0,), (0,)), ((), ()))
LANES = 128


def split(value):
    high = value.astype(BF16)
    low = (value - high.astype(F32)).astype(BF16)
    return high, low


def dot(a, b, dims=ROWS_COLS):
    return lax.dot_general(a, b, dims, preferred_element_type=F32)


def dot3(a, b, dims=ROWS_COLS):
    return dot(a[0], b[0], dims) + (dot(a[0], b[1], dims) + dot(a[1], b[0], dims))


def layer_norm(values, scales):
    average = jnp.mean(values, axis=-1, keepdims=True)
    centered = values - average
    variance = jnp.mean(centered * centered, axis=-1, keepdims=True)
    return centered * lax.rsqrt(variance + 1e-05) * scales


def kernel(
    n_seq, n_res, heads,
    align_ref, pair_ref, outer_gain_ref, w_in_ref, w_out_ref, pair_gain_ref, w_bias_ref,
    row_gain_ref, w_project_ref, w_output_ref,
    out_ref, pair_out_ref,
    maps, left, right3, rows, w_pair, w_proj, w_outp, update, partial, total, bias,
    q_buf, k_buf, v_buf, gate, done,
    left_s, left_r, rows_s, rows_r, sum_s, sum_r, b1_s, b1_r, b2_s, b2_r, out_s, out_r,
):
    seqs, res, cm = align_ref.shape
    row_block = pair_ref.shape[0]
    cz = pair_ref.shape[2]
    chan = w_in_ref.shape[1] // 2
    group = seqs // n_res
    total_res = res * n_res
    head = cm // heads
    width = res * chan
    tile_rows = row_block * res
    my_seq = lax.axis_index("seq")
    me = lax.axis_index("res")

    barrier = pltpu.get_barrier_semaphore()
    for t in range(1, n_res):
        pl.semaphore_signal(
            barrier, inc=1, device_id=(my_seq, lax.rem(me + t, n_res)), device_id_type=MESH
        )
    for t in range(1, n_seq):
        pl.semaphore_signal(
            barrier, inc=1, device_id=(lax.rem(my_seq + t, n_seq), me), device_id_type=MESH
        )

    def res_copy(src, dst, send, recv, peer):
        return pltpu.make_async_remote_copy(
            src_ref=src, dst_ref=dst, send_sem=send, recv_sem=recv,
            device_id=(my_seq, peer), device_id_type=MESH,
        )

    def seq_copy(src, dst, send, recv, peer):
        return pltpu.make_async_remote_copy(
            src_ref=src, dst_ref=dst, send_sem=send, recv_sem=recv,
            device_id=(peer, me), device_id_type=MESH,
        )

    normed = layer_norm(align_ref[...], outer_gain_ref[...]).reshape(seqs * res, cm)
    maps[:, : 2 * chan] = dot3(split(normed), split(w_in_ref[...]))
    source = lax.broadcasted_iota(jnp.int32, (2 * chan, 2 * width), 0)
    column = lax.broadcasted_iota(jnp.int32, (2 * chan, 2 * width), 1)
    placed = jnp.zeros((seqs, 2 * width), F32)
    for r in range(res):
        target = jnp.where(source < chan, source * res + r, width + r * chan + source - chan)
        pick = jnp.where(column == target, 1.0, 0.0).astype(BF16)
        high, low = split(maps[pl.ds(r, seqs, stride=res), :][:, : 2 * chan])
        placed = placed + (dot(high, pick) + dot(low, pick))
    left[me] = placed[:, :width]
    r_high, r_low = split(placed[:, width:])
    right3[...] = jnp.concatenate([r_high, r_low, r_high], axis=0)

    pl.semaphore_wait(barrier, n_res - 1 + n_seq - 1)

    def send_left(t, c):
        peer = lax.rem(me + t, n_res)
        res_copy(left.at[me], left.at[me], left_s.at[peer], left_r.at[me], peer).start()
        return c

    def rows_copy(peer, slot):
        return res_copy(
            align_ref.at[pl.ds(peer * group, group)],
            rows.at[:, pl.ds(slot * res, res), :],
            rows_s.at[peer], rows_r.at[slot], peer,
        )

    def send_rows(t, c):
        rows_copy(lax.rem(me + t, n_res), me).start()
        return c

    lax.fori_loop(1, n_res, send_left, 0)
    lax.fori_loop(1, n_res, send_rows, 0)
    rows[:, pl.ds(pl.multiple_of(me * res, res), res), :] = align_ref[pl.ds(me * group, group)]

    for ref, wref in ((w_pair, w_out_ref), (w_proj, w_project_ref), (w_outp, w_output_ref)):
        high, low = split(wref[...])
        ref[0] = high
        ref[1] = low

    per = LANES // chan
    lane = lax.broadcasted_iota(jnp.int32, (1, LANES), 1) // chan

    def outer_step(src):
        high, low = split(left[src])
        product = dot(jnp.concatenate([high, high, low], axis=0), right3[...], COLS_COLS)
        parts = product.reshape(chan // per, per, res, width)
        blocks = []
        for j in range(res):
            base = (j // per) * LANES
            acc = None
            for q in range(per):
                piece = parts[:, q, :, base : base + LANES].reshape(-1, LANES)
                shift = ((q - j % per) * chan) % LANES
                if shift:
                    piece = pltpu.roll(piece, shift, 1)
                acc = piece if acc is None else jnp.where(lane == q, piece, acc)
            blocks.append(
                jnp.concatenate([acc[g * res : (g + 1) * res] for g in range(chan // per)], axis=1)
            )
        flat = jnp.concatenate(blocks, axis=0)
        update[pl.ds(pl.multiple_of(src * res * res, res * res), res * res), :] = dot3(
            split(flat), (w_pair[0], w_pair[1])
        )

    def outer_loop(t, c):
        src = lax.rem(me + n_res - t, n_res)
        @pl.when(t > 0)
        def _():
            res_copy(left.at[me], left.at[src], left_s.at[src], left_r.at[src], src).wait_recv()
        outer_step(src)
        return c

    lax.fori_loop(0, n_res, outer_loop, 0)

    def sum_copy(peer, slot):
        return seq_copy(
            update.at[pl.ds(pl.multiple_of(peer * tile_rows, tile_rows), tile_rows)],
            partial.at[slot], sum_s.at[peer], sum_r.at[slot], peer,
        )

    for t in range(1, n_seq):
        sum_copy(lax.rem(my_seq + t, n_seq), my_seq).start()
    summed = update[pl.ds(pl.multiple_of(my_seq * tile_rows, tile_rows), tile_rows), :]
    for t in range(1, n_seq):
        src = lax.rem(my_seq + n_seq - t, n_seq)
        sum_copy(src, src).wait_recv()
        summed = summed + partial[src]
    total[...] = summed * (1.0 / (seqs * n_seq))

    lane_row = lax.broadcasted_iota(jnp.int32, (res, heads * row_block), 1) % row_block
    expand_h = lax.broadcasted_iota(jnp.int32, (heads, heads * row_block), 0)
    expand_l = lax.broadcasted_iota(jnp.int32, (heads, heads * row_block), 1)
    expand = jnp.where(expand_l // row_block == expand_h, 1.0, 0.0)
    w_rep = lax.dot_general(
        w_bias_ref[...], expand, ROWS_COLS,
        precision=lax.Precision.HIGHEST, preferred_element_type=F32,
    )
    tiles = []
    for i in range(row_block):
        start = (i // res) * res * res + i % res
        tile = pair_ref[i] + total[pl.ds(start, res, stride=res), :]
        pair_out_ref[i] = tile
        tiles.append(layer_norm(tile, pair_gain_ref[...]))
    spread = lax.dot_general(
        jnp.concatenate(tiles, axis=0), w_rep, ROWS_COLS,
        precision=lax.Precision.HIGHEST, preferred_element_type=F32,
    )
    tile_bias = jnp.zeros((res, heads * row_block), F32)
    for i in range(row_block):
        tile_bias = jnp.where(lane_row == i, spread[i * res : (i + 1) * res], tile_bias)
    bias[my_seq, pl.ds(pl.multiple_of(me * res, res), res), :] = tile_bias

    def bias_copy(peer, slot):
        return res_copy(
            bias.at[my_seq, pl.ds(pl.multiple_of(me * res, res), res)],
            bias.at[my_seq, pl.ds(pl.multiple_of(slot * res, res), res)],
            b1_s.at[peer], b1_r.at[slot], peer,
        )

    def send_bias(t, c):
        bias_copy(lax.rem(me + t, n_res), me).start()
        return c

    lax.fori_loop(1, n_res, send_bias, 0)

    def wait_rows(t, c):
        src = lax.rem(me + n_res - t, n_res)
        rows_copy(src, src).wait_recv()
        return c

    lax.fori_loop(1, n_res, wait_rows, 0)

    def project(s, c):
        parts = split(layer_norm(rows[s], row_gain_ref[...]))
        mapped = dot3(parts, (w_proj[0], w_proj[1]))
        for buf, k in ((q_buf, 0), (k_buf, 1), (v_buf, 2)):
            value = mapped[:, k * cm : (k + 1) * cm]
            if k == 0:
                value = value * head ** (-0.5)
            high, low = split(value)
            buf[0, s] = high
            buf[1, s] = low
        gate[s] = jax.nn.sigmoid(mapped[:, 3 * cm :])
        return c

    half = group // 2
    lax.fori_loop(0, half, project, 0)

    def wait_bias(t, c):
        src = lax.rem(me + n_res - t, n_res)
        bias_copy(src, src).wait_recv()
        return c

    lax.fori_loop(1, n_res, wait_bias, 0)

    def bias2_copy(peer, slot):
        return seq_copy(bias.at[my_seq], bias.at[slot], b2_s.at[peer], b2_r.at[slot], peer)

    for t in range(1, n_seq):
        bias2_copy(lax.rem(my_seq + t, n_seq), my_seq).start()
    lax.fori_loop(half, group, project, 0)
    for t in range(1, n_seq):
        src = lax.rem(my_seq + n_seq - t, n_seq)
        bias2_copy(src, src).wait_recv()

    channel_head = lax.broadcasted_iota(jnp.int32, (row_block, cm), 1) // head

    def out_copy(s, peer, slot, to):
        return res_copy(
            done.at[s, pl.ds(pl.multiple_of(peer * res, res), res)],
            out_ref.at[slot * group + s],
            out_s.at[s, peer], out_r.at[s, slot], to,
        )

    def attend(s, c):
        keys = (k_buf[0, s], k_buf[1, s])
        v_high, v_low = v_buf[0, s], v_buf[1, s]
        values3 = jnp.concatenate([v_high, v_low, v_high], axis=0)
        mixed = []
        for a in range(n_seq):
            stacked = []
            for k in range(2):
                block = q_buf[k, s, a * row_block : (a + 1) * row_block, :]
                stacked.append(
                    jnp.concatenate(
                        [jnp.where(channel_head == h, block, jnp.zeros_like(block))
                         for h in range(heads)], axis=0)
                )
            scores = dot3(keys, stacked, ROWS_ROWS) + bias[a]
            peak = jnp.max(scores, axis=0, keepdims=True)
            powers = jnp.exp(scores - peak)
            weights = powers / jnp.sum(powers, axis=0, keepdims=True)
            p_high, p_low = split(weights)
            blended = dot(jnp.concatenate([p_high, p_high, p_low], axis=0), values3, COLS_COLS)
            acc = blended[:row_block]
            for h in range(1, heads):
                acc = jnp.where(
                    channel_head == h, blended[h * row_block : (h + 1) * row_block], acc
                )
            mixed.append(acc)
        gated = gate[s] * jnp.concatenate(mixed, axis=0)
        done[s] = rows[s] + dot3(split(gated), (w_outp[0], w_outp[1]))
        out_ref[me * group + s] = done[s, pl.ds(pl.multiple_of(me * res, res), res), :]

        def send_out(t, d):
            peer = lax.rem(me + t, n_res)
            out_copy(s, peer, me, peer).start()
            return d

        lax.fori_loop(1, n_res, send_out, 0)
        return c

    lax.fori_loop(0, group, attend, 0)

    def finish(t, c):
        src = lax.rem(me + n_res - t, n_res)

        def finish_one(s, d):
            out_copy(s, src, src, src).wait()
            return d

        lax.fori_loop(0, group, finish_one, 0)
        res_copy(left.at[me], left.at[src], left_s.at[src], left_r.at[src], src).wait_send()
        rows_copy(src, src).wait_send()
        bias_copy(src, src).wait_send()
        return c

    lax.fori_loop(1, n_res, finish, 0)
    for t in range(1, n_seq):
        src = lax.rem(my_seq + n_seq - t, n_seq)
        sum_copy(src, src).wait_send()
        bias2_copy(src, src).wait_send()


def on_device(n_seq, n_res, *args):
    align, pair, _, w_in, w_out, _, w_bias, _, w_project, w_output = args
    seqs, res, cm = align.shape
    row_block, _, cz = pair.shape
    heads = w_bias.shape[1]
    chan = w_in.shape[1] // 2
    group = seqs // n_res
    total_res = res * n_res
    width = res * chan
    vmem = pl.BlockSpec(memory_space=pltpu.VMEM)
    dma = pltpu.SemaphoreType.DMA
    scratch = [
        pltpu.VMEM((seqs * res, LANES), F32),
        pltpu.VMEM((n_res, seqs, width), F32),
        pltpu.VMEM((3 * seqs, width), BF16),
        pltpu.VMEM((group, total_res, cm), F32),
        pltpu.VMEM((2,) + w_out.shape, BF16),
        pltpu.VMEM((2,) + w_project.shape, BF16),
        pltpu.VMEM((2,) + w_output.shape, BF16),
        pltpu.VMEM((total_res * res, cz), F32),
        pltpu.VMEM((n_seq, row_block * res, cz), F32),
        pltpu.VMEM((row_block * res, cz), F32),
        pltpu.VMEM((n_seq, total_res, heads * row_block), F32),
        pltpu.VMEM((2, group, total_res, cm), BF16),
        pltpu.VMEM((2, group, total_res, cm), BF16),
        pltpu.VMEM((2, group, total_res, cm), BF16),
        pltpu.VMEM((group, total_res, cm), F32),
        pltpu.VMEM((group, total_res, cm), F32),
        dma((n_res,)), dma((n_res,)), dma((n_res,)), dma((n_res,)),
        dma((n_seq,)), dma((n_seq,)), dma((n_res,)), dma((n_res,)),
        dma((n_seq,)), dma((n_seq,)), dma((group, n_res)), dma((group, n_res)),
    ]
    vectors = [a.reshape(1, -1) if a.ndim == 1 else a for a in args]
    return pl.pallas_call(
        functools.partial(kernel, n_seq, n_res, heads),
        out_shape=(
            jax.ShapeDtypeStruct(align.shape, F32),
            jax.ShapeDtypeStruct(pair.shape, F32),
        ),
        in_specs=[vmem] * len(args),
        out_specs=(vmem, vmem),
        scratch_shapes=scratch,
        compiler_params=pltpu.CompilerParams(
            collective_id=0, has_side_effects=True, vmem_limit_bytes=60 * 1024 * 1024
        ),
    )(*vectors)


def solution(mesh):
    tiled = P("seq", "res", None)
    return jax.shard_map(
        functools.partial(on_device, mesh.shape["seq"], mesh.shape["res"]),
        mesh=mesh,
        in_specs=(tiled, tiled) + (P(),) * 8,
        out_specs=(tiled, tiled),
        check_vma=False,
    )
```

time: 150 us -> 63.6 us (0.42)
  blocking collectives: 86.8 us -> 0 us
  Pallas kernels: 0 us -> 58.1 us
  matrix products: 20.3 us -> 0 us
  local copies, waits for them, and re-layouts: 23.6 us -> 4.69 us
  other arithmetic: 9.14 us -> 0 us
  starting transfers between devices: 8.05 us -> 0 us
    all_gather x4 -> x0, blocking collectives: 67 us -> none  [the longest x1 25.1 us: on_device(): left_all = lax.all_gather(left_maps, 'res', axis=2, tiled=True)]
    pallas_call x0 -> x1, Pallas kernels: none -> 58.1 us  [on_device(): pl.pallas_call(functools.partial(kernel, n_seq, n_res, heads), out_shape=...]
    dot_general x8 -> x0, matrix products: 20.3 us -> none  [the longest x1 5.09 us: row_attention(): jnp.einsum('ihd,jhd->hij', query_map, key_map, precision=precise) + bias_all]
    all_to_all x1 -> x0, blocking collectives: 19.8 us -> none  [on_device(): lax.all_to_all(attended, 'res', split_axis=2, concat_axis=0, tiled=True)]
    all_to_all x2 -> x0, starting transfers between devices: 8.05 us -> none  [the longest x1 4.34 us: on_device(): lax.all_to_all(sequence_grouped_rows, 'res', split_axis=0, concat_axis=2,...]
    reduce_sum x6 -> x0, other arithmetic: 5.73 us -> none  [the longest x3 2.73 us: layer_norm(): variance = jnp.mean(centered * centered, axis=-1, keepdims=True)]
    slice x3 -> x0, local copies, waits for them, and re-layouts: 4.91 us -> none  [the longest x1 2.41 us: row_attention(): projected[:, channels:2 * channels].reshape(residues, head_count, head_size)]
    div x4 -> x0, local copies, waits for them, and re-layouts: 4.09 us -> none  [the longest x2 4 us: on_device(): summed / seq_total]
  transfers between devices with their start and end apart: 2 -> 0, of which waited for: 0 -> 0; matrix products, arithmetic and copies ran while one was open for 10% -> 0% of each run, Pallas kernels for 0% -> 0%
where the time goes in v1:
time: 63.6 us; the launch traced here: 63.4 us
  Pallas kernels  58.1 us (91%)
  local copies, waits for them, and re-layouts  4.69 us (7%)
  between operations  0.66 us (1%)
    pallas_call x1, Pallas kernels, on_device(): pl.pallas_call(functools.partial(kernel, n_seq, n_res, heads), out_shape=...  58.1 us
    unnamed x10, local copies, waits for them, and re-layouts  4.69 us

profile of v1, /device:TPU:0, one launch (start us, length us, event | category | flops | bytes accessed | tf_op | source)
XLA Modules:
  0.0 63.4 jit_solution(9491330721570780543)
XLA Ops:
  0.6 0.0 copy-start.2
  0.6 0.0 copy-start
  0.6 0.7 %copy-done.2 = f32[128,8]{0,1:T(8,128)S(1)} copy-done((f32[128,8]{0,1:T(8,128)S(1)}, f32[128,8]{0,1:T(8,128)}, u32[]{:S(2)}) %copy-start.2) | copy-done | bytes 4120
  1.3 0.7 %copy.13.w_bias_ref = f32[128,8]{1,0:T(8,128)} copy(f32[128,8]{0,1:T(8,128)S(1)} %copy-done.2) | data formatting | bytes 8192 | tf_op args[6]
  2.0 0.0 copy-done
  2.0 0.8 %copy.12.w_in_ref = f32[256,64]{1,0:T(8,128)} copy(f32[256,64]{0,1:T(8,128)S(1)} %copy-done) | data formatting | bytes 131072 | tf_op args[3]
  2.8 58.1 %shard_map.113 = (f32[64,8,256]{2,1,0:T(8,128)}, f32[16,8,128]{2,1,0:T(8,128)}) custom-call(f32[64,8,256]{2,1,0:T(8,128)} %align_ref.1, f32[16,8,128]{2,1,0:T(8,128)} %pair_ref.1, f32[1,256]{1,0:T(1,128)} %bitcast.3, f32[256,64]{1,0:T(8,128)} %copy.12.w_in_ref, f32[1024,128]{1,0:T(8,128)} %w_out_ref.1, f32[1,128]{1,0:T(1,128)} %bitcast.5, ...), custom_call_target="tpu_custom_call" | custom-call | tf_op jit(solution)/shard_map/pallas_call | solution.py:351
  60.9 0.0 copy-start.1
  60.9 1.9 %copy.16 = f32[64,8,256]{2,1,0:T(8,128)} copy(f32[64,8,256]{2,1,0:T(8,128)} %get-tuple-element.4) | data formatting | bytes 1048576
  62.8 0.0 copy-done.1
  62.8 0.6 copy.17
Async XLA Ops:
  0.6 0.7 %copy-start.2 = (f32[128,8]{0,1:T(8,128)S(1)}, f32[128,8]{0,1:T(8,128)}, u32[]{:S(2)}) copy-start(f32[128,8]{0,1:T(8,128)} %param.16) | copy-start | bytes 12292
  0.6 1.4 %copy-start = (f32[256,64]{0,1:T(8,128)S(1)}, f32[256,64]{0,1:T(8,128)}, u32[]{:S(2)}) copy-start(f32[256,64]{0,1:T(8,128)} %param.13) | copy-start | bytes 196612
  60.9 1.9 %copy-start.1 = (f32[16,8,128]{2,1,0:T(8,128)S(1)}, f32[16,8,128]{2,1,0:T(8,128)}, u32[]{:S(2)}) copy-start(f32[16,8,128]{2,1,0:T(8,128)} %get-tuple-element.5) | copy-start | bytes 196612

commit v2 on v1

v2 whole, which is shorter than its diff:
```python
import functools
import jax
import jax.numpy as jnp
from jax import lax
from jax.experimental import pallas as pl
from jax.experimental.pallas import tpu as pltpu
from jax.sharding import PartitionSpec as P

F32 = jnp.float32
BF16 = jnp.bfloat16
MESH = pl.DeviceIdType.MESH
ROWS_COLS = (((1,), (0,)), ((), ()))
ROWS_ROWS = (((1,), (1,)), ((), ()))
COLS_COLS = (((0,), (0,)), ((), ()))
LANES = 128
PAIR = 2
CHUNK = 4


def split(value):
    high = value.astype(BF16)
    low = (value - high.astype(F32)).astype(BF16)
    return high, low


def dot(a, b, dims=ROWS_COLS):
    return lax.dot_general(a, b, dims, preferred_element_type=F32)


def dot3(a, b, dims=ROWS_COLS):
    return dot(a[0], b[0], dims) + (dot(a[0], b[1], dims) + dot(a[1], b[0], dims))


def layer_norm(values, scales):
    average = jnp.mean(values, axis=-1, keepdims=True)
    centered = values - average
    variance = jnp.mean(centered * centered, axis=-1, keepdims=True)
    return centered * lax.rsqrt(variance + 1e-05) * scales


def kernel(
    n_seq, n_res, heads,
    align_ref, pair_ref, outer_gain_ref, w_in_ref, w_out_ref, pair_gain_ref, w_bias_ref,
    row_gain_ref, w_project_ref, w_output_ref,
    out_ref, pair_out_ref,
    maps, left, right, right3, rows, w_pair, w_proj, w_outp, update, partial, total, bias,
    q_buf, k_buf, v_buf, gate, done, w_out_v, w_project_v, w_output_v,
    left_s, left_r, right_s, right_r, rows_s, rows_r, sum_s, sum_r, bias_s, bias_r,
    out_s, out_r, load_s,
):
    seqs, res, cm = align_ref.shape
    row_block = pair_ref.shape[0]
    cz = pair_ref.shape[2]
    chan = w_in_ref.shape[0] // 2
    group = seqs // n_res
    total_res = res * n_res
    head = cm // heads
    width = res * chan
    devices = n_seq * n_res
    chips = n_res // PAIR
    part_rows = res * res
    my_seq = lax.axis_index("seq")
    me = lax.axis_index("res")

    barrier = pltpu.get_barrier_semaphore()
    mine = my_seq * n_res + me
    core = lax.rem(me, PAIR)
    chip = me // PAIR
    sibling = chip * PAIR + 1 - core

    def greet(t, c):
        other = lax.rem(mine + t, devices)
        pl.semaphore_signal(
            barrier, inc=1, device_id=(other // n_res, lax.rem(other, n_res)), device_id_type=MESH
        )
        return c

    lax.fori_loop(1, devices, greet, 0)
    loads = [
        pltpu.make_async_copy(hbm, held, load_s.at[k])
        for k, (hbm, held) in enumerate(
            ((w_out_ref, w_out_v), (w_project_ref, w_project_v), (w_output_ref, w_output_v))
        )
    ]
    for load in loads:
        load.start()

    def res_copy(src, dst, send, recv, peer):
        return pltpu.make_async_remote_copy(
            src_ref=src, dst_ref=dst, send_sem=send, recv_sem=recv,
            device_id=(my_seq, peer), device_id_type=MESH,
        )

    def any_copy(src, dst, send, recv, seq, peer):
        return pltpu.make_async_remote_copy(
            src_ref=src, dst_ref=dst, send_sem=send, recv_sem=recv,
            device_id=(seq, peer), device_id_type=MESH,
        )

    normed = layer_norm(align_ref[...], outer_gain_ref[...]).reshape(seqs * res, cm)
    maps[:, : 2 * chan] = dot3(split(normed), split(w_in_ref[...]), ROWS_ROWS)
    source = lax.broadcasted_iota(jnp.int32, (2 * chan, 2 * width), 0)
    column = lax.broadcasted_iota(jnp.int32, (2 * chan, 2 * width), 1)
    placed = jnp.zeros((seqs, 2 * width), F32)
    for r in range(res):
        target = jnp.where(source < chan, source * res + r, width + r * chan + source - chan)
        pick = jnp.where(column == target, 1.0, 0.0).astype(BF16)
        high, low = split(maps[pl.ds(r, seqs, stride=res), :][:, : 2 * chan])
        placed = placed + (dot(high, pick) + dot(low, pick))
    left[chip] = placed[:, :width]
    right[core] = placed[:, width:]

    pl.semaphore_wait(barrier, devices - 1)

    def left_copy(to, slot):
        return res_copy(
            left.at[chip], left.at[slot], left_s.at[to], left_r.at[slot], to * PAIR + core
        )

    def send_left(t, c):
        left_copy(lax.rem(chip + t, chips), chip).start()
        return c

    def right_copy(slot):
        return res_copy(
            right.at[core], right.at[slot], right_s.at[0], right_r.at[0], sibling
        )

    right_copy(core).start()
    lax.fori_loop(1, chips, send_left, 0)

    def rows_copy(peer, slot):
        return res_copy(
            align_ref.at[pl.ds(peer * group, group)],
            rows.at[:, pl.ds(slot * res, res), :],
            rows_s.at[peer], rows_r.at[slot], peer,
        )

    def send_rows(t, c):
        rows_copy(lax.rem(me + t, n_res), me).start()
        return c

    lax.fori_loop(1, n_res, send_rows, 0)
    rows[:, pl.ds(pl.multiple_of(me * res, res), res), :] = align_ref[pl.ds(me * group, group)]

    for load in loads:
        load.wait()
    for ref, wref in ((w_pair, w_out_v), (w_proj, w_project_v), (w_outp, w_output_v)):
        high, low = split(wref[...])
        ref[0] = high
        ref[1] = low

    right_copy(1 - core).wait_recv()
    both = jnp.concatenate([right[k] for k in range(PAIR)], axis=1)
    r_high, r_low = split(both)
    right3[...] = jnp.concatenate([r_high, r_low, r_high], axis=0)
    per = LANES // chan
    lane = lax.broadcasted_iota(jnp.int32, (1, LANES), 1) // chan

    def outer_step(src):
        high, low = split(left[src])
        product = dot(jnp.concatenate([high, high, low], axis=0), right3[...], COLS_COLS)
        parts = product.reshape(chan // per, per, res, PAIR * width)
        blocks = []
        for j in range(PAIR * res):
            base = (j // per) * LANES
            acc = None
            for q in range(per):
                piece = parts[:, q, :, base : base + LANES].reshape(-1, LANES)
                shift = ((q - j % per) * chan) % LANES
                if shift:
                    piece = pltpu.roll(piece, shift, 1)
                acc = piece if acc is None else jnp.where(lane == q, piece, acc)
            blocks.append(
                jnp.concatenate([acc[g * res : (g + 1) * res] for g in range(chan // per)], axis=1)
            )
        flat = jnp.concatenate(blocks, axis=0)
        summed_pair = dot3(
            split(flat), (w_pair[0], w_pair[1])
        )
        for k in range(PAIR):
            update[src, k] = summed_pair[k * part_rows : (k + 1) * part_rows]

    def sum_copy(owner, k, slot_seq, slot_core):
        return any_copy(
            update.at[owner, k], partial.at[slot_seq, slot_core],
            sum_s.at[owner, k], sum_r.at[slot_seq, slot_core], owner, chip * PAIR + k,
        )

    def outer_loop(t, c):
        src = lax.rem(chip + chips - t, chips)
        @pl.when(t > 0)
        def _():
            left_copy(src, src).wait_recv()
        outer_step(src)
        for k in range(PAIR):
            @pl.when(jnp.logical_or(src != my_seq, core != k))
            def _():
                sum_copy(src, k, my_seq, core).start()
        return c

    lax.fori_loop(0, chips, outer_loop, 0)

    partial[my_seq, core] = update[my_seq, core]
    for a in range(n_seq):
        for k in range(PAIR):
            @pl.when(jnp.logical_or(a != my_seq, core != k))
            def _():
                sum_copy(a, k, a, k).wait_recv()
    summed = jnp.concatenate(
        [functools.reduce(jnp.add, [partial[a, k] for a in range(n_seq)]) for k in range(PAIR)],
        axis=0,
    )
    total[...] = summed * (1.0 / (seqs * n_seq))

    lane_row = lax.broadcasted_iota(jnp.int32, (res, heads * row_block), 1) % row_block
    expand_h = lax.broadcasted_iota(jnp.int32, (heads, heads * row_block), 0)
    expand_l = lax.broadcasted_iota(jnp.int32, (heads, heads * row_block), 1)
    expand = jnp.where(expand_l // row_block == expand_h, 1.0, 0.0)
    w_rep = lax.dot_general(
        w_bias_ref[...], expand, COLS_COLS,
        precision=lax.Precision.HIGHEST, preferred_element_type=F32,
    )
    tiles = []
    for i in range(row_block):
        start = (i // res) * res * res + i % res
        tile = pair_ref[i] + total[pl.ds(start, res, stride=res), :]
        pair_out_ref[i] = tile
        tiles.append(layer_norm(tile, pair_gain_ref[...]))
    spread = lax.dot_general(
        jnp.concatenate(tiles, axis=0), w_rep, ROWS_COLS,
        precision=lax.Precision.HIGHEST, preferred_element_type=F32,
    )
    tile_bias = jnp.zeros((res, heads * row_block), F32)
    for i in range(row_block):
        tile_bias = jnp.where(lane_row == i, spread[i * res : (i + 1) * res], tile_bias)
    bias[my_seq, pl.ds(pl.multiple_of(me * res, res), res), :] = tile_bias

    def bias_copy(other, slot):
        place = bias.at[slot // n_res, pl.ds(pl.multiple_of(lax.rem(slot, n_res) * res, res), res)]
        own = bias.at[my_seq, pl.ds(pl.multiple_of(me * res, res), res)]
        return any_copy(
            own, place, bias_s.at[other], bias_r.at[slot], other // n_res, lax.rem(other, n_res)
        )

    def send_bias(t, c):
        bias_copy(lax.rem(mine + t, devices), mine).start()
        return c

    lax.fori_loop(1, devices, send_bias, 0)

    def wait_rows(t, c):
        src = lax.rem(me + n_res - t, n_res)
        rows_copy(src, src).wait_recv()
        return c

    lax.fori_loop(1, n_res, wait_rows, 0)

    def project(s, c):
        parts = split(layer_norm(rows[s], row_gain_ref[...]))
        mapped = dot3(parts, (w_proj[0], w_proj[1]))
        for buf, k in ((q_buf, 0), (k_buf, 1), (v_buf, 2)):
            value = mapped[:, k * cm : (k + 1) * cm]
            if k == 0:
                value = value * head ** (-0.5)
            high, low = split(value)
            buf[0, s] = high
            buf[1, s] = low
        gate[s] = jax.nn.sigmoid(mapped[:, 3 * cm :])
        return c

    lax.fori_loop(0, group, project, 0)

    def wait_bias(t, c):
        src = lax.rem(mine + devices - t, devices)
        bias_copy(src, src).wait_recv()
        return c

    lax.fori_loop(1, devices, wait_bias, 0)

    channel_head = lax.broadcasted_iota(jnp.int32, (row_block, cm), 1) // head

    def out_copy(s, peer, slot, to):
        return res_copy(
            done.at[s, pl.ds(pl.multiple_of(peer * res, res), res)],
            out_ref.at[slot * group + s],
            out_s.at[s, peer], out_r.at[s, slot], to,
        )

    def attend(s, c):
        keys = (k_buf[0, s], k_buf[1, s])
        v_high, v_low = v_buf[0, s], v_buf[1, s]
        values3 = jnp.concatenate([v_high, v_low, v_high], axis=0)
        mixed = []
        for a0 in range(0, n_seq, CHUNK):
            chunk = range(a0, min(a0 + CHUNK, n_seq))
            stacked = [
                jnp.concatenate(
                    [jnp.where(channel_head == h, block, jnp.zeros_like(block))
                     for block in [q_buf[k, s, a * row_block : (a + 1) * row_block, :] for a in chunk]
                     for h in range(heads)], axis=0)
                for k in range(2)
            ]
            scores = dot3(keys, stacked, ROWS_ROWS) + jnp.concatenate([bias[a] for a in chunk], axis=1)
            peak = jnp.max(scores, axis=0, keepdims=True)
            powers = jnp.exp(scores - peak)
            weights = powers / jnp.sum(powers, axis=0, keepdims=True)
            p_high, p_low = split(weights)
            blended = dot(jnp.concatenate([p_high, p_high, p_low], axis=0), values3, COLS_COLS)
            for n in range(len(chunk)):
                base = n * heads * row_block
                acc = blended[base : base + row_block]
                for h in range(1, heads):
                    low = base + h * row_block
                    acc = jnp.where(channel_head == h, blended[low : low + row_block], acc)
                mixed.append(acc)
        gated = gate[s] * jnp.concatenate(mixed, axis=0)
        done[s] = rows[s] + dot3(split(gated), (w_outp[0], w_outp[1]))
        out_ref[me * group + s] = done[s, pl.ds(pl.multiple_of(me * res, res), res), :]

        def send_out(t, d):
            peer = lax.rem(me + t, n_res)
            out_copy(s, peer, me, peer).start()
            return d

        lax.fori_loop(1, n_res, send_out, 0)
        return c

    lax.fori_loop(0, group, attend, 0)

    def finish(t, c):
        src = lax.rem(me + n_res - t, n_res)

        def finish_one(s, d):
            out_copy(s, src, src, src).wait()
            return d

        lax.fori_loop(0, group, finish_one, 0)
        rows_copy(src, src).wait_send()
        return c

    lax.fori_loop(1, n_res, finish, 0)

    def finish_left(t, c):
        left_copy(lax.rem(chip + t, chips), chip).wait_send()
        return c

    lax.fori_loop(1, chips, finish_left, 0)
    right_copy(core).wait_send()
    for a in range(n_seq):
        for k in range(PAIR):
            @pl.when(jnp.logical_or(a != my_seq, core != k))
            def _():
                sum_copy(a, k, my_seq, core).wait_send()

    def finish_bias(t, c):
        bias_copy(lax.rem(mine + t, devices), mine).wait_send()
        return c

    lax.fori_loop(1, devices, finish_bias, 0)


def on_device(n_seq, n_res, *args):
    align, pair, _, w_in, w_out, _, w_bias, _, w_project, w_output = args
    seqs, res, cm = align.shape
    row_block, _, cz = pair.shape
    heads = w_bias.shape[1]
    chan = w_in.shape[1] // 2
    assert row_block == PAIR * res and n_res == PAIR * n_seq
    chips = n_res // PAIR
    group = seqs // n_res
    total_res = res * n_res
    width = res * chan
    vmem = pl.BlockSpec(memory_space=pltpu.VMEM)
    dma = pltpu.SemaphoreType.DMA
    scratch = [
        pltpu.VMEM((seqs * res, LANES), F32),
        pltpu.VMEM((chips, seqs, width), F32),
        pltpu.VMEM((PAIR, seqs, width), F32),
        pltpu.VMEM((3 * seqs, PAIR * width), BF16),
        pltpu.VMEM((group, total_res, cm), F32),
        pltpu.VMEM((2,) + w_out.shape, BF16),
        pltpu.VMEM((2,) + w_project.shape, BF16),
        pltpu.VMEM((2,) + w_output.shape, BF16),
        pltpu.VMEM((chips, PAIR, res * res, cz), F32),
        pltpu.VMEM((n_seq, PAIR, res * res, cz), F32),
        pltpu.VMEM((row_block * res, cz), F32),
        pltpu.VMEM((n_seq, total_res, heads * row_block), F32),
        pltpu.VMEM((2, group, total_res, cm), BF16),
        pltpu.VMEM((2, group, total_res, cm), BF16),
        pltpu.VMEM((2, group, total_res, cm), BF16),
        pltpu.VMEM((group, total_res, cm), F32),
        pltpu.VMEM((group, total_res, cm), F32),
        pltpu.VMEM(w_out.shape, F32),
        pltpu.VMEM(w_project.shape, F32),
        pltpu.VMEM(w_output.shape, F32),
        dma((chips,)), dma((chips,)), dma((1,)), dma((1,)), dma((n_res,)), dma((n_res,)),
        dma((n_seq, PAIR)), dma((n_seq, PAIR)), dma((n_seq * n_res,)), dma((n_seq * n_res,)),
        dma((group, n_res)), dma((group, n_res)), dma((3,)),
    ]
    vectors = [a.reshape(1, -1) if a.ndim == 1 else a for a in args]
    vectors[3] = w_in.T
    vectors[6] = w_bias.T
    hbm = pl.BlockSpec(memory_space=pl.ANY)
    return pl.pallas_call(
        functools.partial(kernel, n_seq, n_res, heads),
        out_shape=(
            jax.ShapeDtypeStruct(align.shape, F32),
            jax.ShapeDtypeStruct(pair.shape, F32),
        ),
        in_specs=[hbm if k in (4, 8, 9) else vmem for k in range(len(args))],
        out_specs=(vmem, vmem),
        scratch_shapes=scratch,
        compiler_params=pltpu.CompilerParams(
            collective_id=0, has_side_effects=True, vmem_limit_bytes=60 * 1024 * 1024
        ),
    )(*vectors)


def solution(mesh):
    tiled = P("seq", "res", None)
    return jax.shard_map(
        functools.partial(on_device, mesh.shape["seq"], mesh.shape["res"]),
        mesh=mesh,
        in_specs=(tiled, tiled) + (P(),) * 8,
        out_specs=(tiled, tiled),
        check_vma=False,
    )
```

time: 63.6 us -> 52.8 us (0.83)
  Pallas kernels: 58.1 us -> 49.5 us
  local copies, waits for them, and re-layouts: 4.69 us -> 2.53 us
    pallas_call x1, Pallas kernels: 58.1 us -> 49.5 us  [on_device(): pl.pallas_call(functools.partial(kernel, n_seq, n_res, heads), out_shape=...]
    unnamed x10 -> x4, local copies, waits for them, and re-layouts: 4.69 us -> 2.53 us
where the time goes in v2:
time: 52.8 us; the launch traced here: 52.6 us
  Pallas kernels  49.5 us (94%)
  local copies, waits for them, and re-layouts  2.53 us (5%)
  between operations  0.65 us (1%)
    pallas_call x1, Pallas kernels, on_device(): pl.pallas_call(functools.partial(kernel, n_seq, n_res, heads), out_shape=...  49.5 us
    unnamed x4, local copies, waits for them, and re-layouts  2.53 us

profile of v2, /device:TPU:0, one launch (start us, length us, event | category | flops | bytes accessed | tf_op | source)
XLA Modules:
  0.0 52.6 jit_solution(10547008008198935982)
XLA Ops:
  0.6 49.5 %shard_map.113 = (f32[64,8,256]{2,1,0:T(8,128)}, f32[16,8,128]{2,1,0:T(8,128)}) custom-call(f32[64,8,256]{2,1,0:T(8,128)} %align_ref.1, f32[16,8,128]{2,1,0:T(8,128)} %pair_ref.1, f32[1,256]{1,0:T(1,128)} %bitcast.7, f32[64,256]{1,0:T(8,128)} %bitcast.5, f32[1024,128]{1,0:T(8,128)} %w_out_ref.1, f32[1,128]{1,0:T(1,128)} %bitcast.9, f32[8,128]{1,0:T(8,128)} %bitcast.6, ...), custom_call_target="tpu_custom_call" | custom-call | tf_op jit(solution)/shard_map/pallas_call | solution.py:405
  50.1 0.0 copy-start
  50.1 1.9 %copy.14 = f32[64,8,256]{2,1,0:T(8,128)} copy(f32[64,8,256]{2,1,0:T(8,128)} %get-tuple-element.4) | data formatting | bytes 1048576
  52.0 0.0 copy-done
  52.0 0.6 %copy.15 = f32[16,8,128]{2,1,0:T(8,128)} copy(f32[16,8,128]{2,1,0:T(8,128)S(1)} %copy-done) | data formatting | bytes 131072
Async XLA Ops:
  50.1 1.9 %copy-start = (f32[16,8,128]{2,1,0:T(8,128)S(1)}, f32[16,8,128]{2,1,0:T(8,128)}, u32[]{:S(2)}) copy-start(f32[16,8,128]{2,1,0:T(8,128)} %get-tuple-element.5) | copy-start | bytes 196612

commit v3 on v2

--- a/solution.py
+++ b/solution.py
@@ -98,6 +98,24 @@
         )
 
     normed = layer_norm(align_ref[...], outer_gain_ref[...]).reshape(seqs * res, cm)
+    half = group // 2
+
+    def rows_copy(peer, slot, part):
+        return res_copy(
+            align_ref.at[pl.ds(peer * group + part * half, half)],
+            rows.at[pl.ds(part * half, half), pl.ds(pl.multiple_of(slot * res, res), res), :],
+            rows_s.at[part, peer], rows_r.at[part, slot], peer,
+        )
+
+    def send_rows(part):
+        def send(t, c):
+            rows_copy(lax.rem(me + t, n_res), me, part).start()
+            return c
+
+        lax.fori_loop(1, n_res, send, 0)
+
+    pl.semaphore_wait(barrier, devices - 1)
+    send_rows(0)
     maps[:, : 2 * chan] = dot3(split(normed), split(w_in_ref[...]), ROWS_ROWS)
     source = lax.broadcasted_iota(jnp.int32, (2 * chan, 2 * width), 0)
     column = lax.broadcasted_iota(jnp.int32, (2 * chan, 2 * width), 1)
@@ -110,8 +128,6 @@
     left[chip] = placed[:, :width]
     right[core] = placed[:, width:]
 
-    pl.semaphore_wait(barrier, devices - 1)
-
     def left_copy(to, slot):
         return res_copy(
             left.at[chip], left.at[slot], left_s.at[to], left_r.at[slot], to * PAIR + core
@@ -129,18 +145,7 @@
     right_copy(core).start()
     lax.fori_loop(1, chips, send_left, 0)
 
-    def rows_copy(peer, slot):
-        return res_copy(
-            align_ref.at[pl.ds(peer * group, group)],
-            rows.at[:, pl.ds(slot * res, res), :],
-            rows_s.at[peer], rows_r.at[slot], peer,
-        )
-
-    def send_rows(t, c):
-        rows_copy(lax.rem(me + t, n_res), me).start()
-        return c
-
-    lax.fori_loop(1, n_res, send_rows, 0)
+    send_rows(1)
     rows[:, pl.ds(pl.multiple_of(me * res, res), res), :] = align_ref[pl.ds(me * group, group)]
 
     for load in loads:
@@ -200,6 +205,30 @@
         return c
 
     lax.fori_loop(0, chips, outer_loop, 0)
+
+    def project(s, c):
+        parts = split(layer_norm(rows[s], row_gain_ref[...]))
+        mapped = dot3(parts, (w_proj[0], w_proj[1]))
+        for buf, k in ((q_buf, 0), (k_buf, 1), (v_buf, 2)):
+            value = mapped[:, k * cm : (k + 1) * cm]
+            if k == 0:
+                value = value * head ** (-0.5)
+            high, low = split(value)
+            buf[0, s] = high
+            buf[1, s] = low
+        gate[s] = jax.nn.sigmoid(mapped[:, 3 * cm :])
+        return c
+
+    def project_part(part):
+        def wait_rows(t, c):
+            src = lax.rem(me + n_res - t, n_res)
+            rows_copy(src, src, part).wait_recv()
+            return c
+
+        lax.fori_loop(1, n_res, wait_rows, 0)
+        lax.fori_loop(part * half, (part + 1) * half, project, 0)
+
+    project_part(0)
 
     partial[my_seq, core] = update[my_seq, core]
     for a in range(n_seq):
@@ -249,27 +278,7 @@
 
     lax.fori_loop(1, devices, send_bias, 0)
 
-    def wait_rows(t, c):
-        src = lax.rem(me + n_res - t, n_res)
-        rows_copy(src, src).wait_recv()
-        return c
-
-    lax.fori_loop(1, n_res, wait_rows, 0)
-
-    def project(s, c):
-        parts = split(layer_norm(rows[s], row_gain_ref[...]))
-        mapped = dot3(parts, (w_proj[0], w_proj[1]))
-        for buf, k in ((q_buf, 0), (k_buf, 1), (v_buf, 2)):
-            value = mapped[:, k * cm : (k + 1) * cm]
-            if k == 0:
-                value = value * head ** (-0.5)
-            high, low = split(value)
-            buf[0, s] = high
-            buf[1, s] = low
-        gate[s] = jax.nn.sigmoid(mapped[:, 3 * cm :])
-        return c
-
-    lax.fori_loop(0, group, project, 0)
+    project_part(1)
 
     def wait_bias(t, c):
         src = lax.rem(mine + devices - t, devices)
@@ -336,7 +345,8 @@
             return d
 
         lax.fori_loop(0, group, finish_one, 0)
-        rows_copy(src, src).wait_send()
+        rows_copy(src, src, 0).wait_send()
+        rows_copy(src, src, 1).wait_send()
         return c
 
     lax.fori_loop(1, n_res, finish, 0)
@@ -369,6 +379,7 @@
     assert row_block == PAIR * res and n_res == PAIR * n_seq
     chips = n_res // PAIR
     group = seqs // n_res
+    assert group % 2 == 0
     total_res = res * n_res
     width = res * chan
     vmem = pl.BlockSpec(memory_space=pltpu.VMEM)
@@ -394,7 +405,7 @@
         pltpu.VMEM(w_out.shape, F32),
         pltpu.VMEM(w_project.shape, F32),
         pltpu.VMEM(w_output.shape, F32),
-        dma((chips,)), dma((chips,)), dma((1,)), dma((1,)), dma((n_res,)), dma((n_res,)),
+        dma((chips,)), dma((chips,)), dma((1,)), dma((1,)), dma((2, n_res)), dma((2, n_res)),
         dma((n_seq, PAIR)), dma((n_seq, PAIR)), dma((n_seq * n_res,)), dma((n_seq * n_res,)),
         dma((group, n_res)), dma((group, n_res)), dma((3,)),
     ]

time: 52.8 us -> 56.4 us (1.068)
  Pallas kernels: 49.5 us -> 53 us
    pallas_call x1, Pallas kernels: 49.5 us -> 53 us  [on_device(): pl.pallas_call(functools.partial(kernel, n_seq, n_res, heads), out_shape=...]
where the time goes in v3:
time: 56.4 us; the launch traced here: 56.2 us
  Pallas kernels  53 us (94%)
  local copies, waits for them, and re-layouts  2.53 us (4%)
  between operations  0.65 us (1%)
    pallas_call x1, Pallas kernels, on_device(): pl.pallas_call(functools.partial(kernel, n_seq, n_res, heads), out_shape=...  53 us
    unnamed x4, local copies, waits for them, and re-layouts  2.53 us

profile of v3, /device:TPU:0, one launch (start us, length us, event | category | flops | bytes accessed | tf_op | source)
XLA Modules:
  0.0 56.2 jit_solution(18028414876086850623)
XLA Ops:
  0.6 53.0 %shard_map.113 = (f32[64,8,256]{2,1,0:T(8,128)}, f32[16,8,128]{2,1,0:T(8,128)}) custom-call(f32[64,8,256]{2,1,0:T(8,128)} %align_ref.1, f32[16,8,128]{2,1,0:T(8,128)} %pair_ref.1, f32[1,256]{1,0:T(1,128)} %bitcast.7, f32[64,256]{1,0:T(8,128)} %bitcast.5, f32[1024,128]{1,0:T(8,128)} %w_out_ref.1, f32[1,128]{1,0:T(1,128)} %bitcast.9, f32[8,128]{1,0:T(8,128)} %bitcast.6, ...), custom_call_target="tpu_custom_call" | custom-call | tf_op jit(solution)/shard_map/pallas_call | solution.py:416
  53.7 0.0 copy-start
  53.7 1.9 %copy.14 = f32[64,8,256]{2,1,0:T(8,128)} copy(f32[64,8,256]{2,1,0:T(8,128)} %get-tuple-element.4) | data formatting | bytes 1048576
  55.6 0.0 copy-done
  55.6 0.6 %copy.15 = f32[16,8,128]{2,1,0:T(8,128)} copy(f32[16,8,128]{2,1,0:T(8,128)S(1)} %copy-done) | data formatting | bytes 131072
Async XLA Ops:
  53.7 1.9 %copy-start = (f32[16,8,128]{2,1,0:T(8,128)S(1)}, f32[16,8,128]{2,1,0:T(8,128)}, u32[]{:S(2)}) copy-start(f32[16,8,128]{2,1,0:T(8,128)} %get-tuple-element.5) | copy-start | bytes 196612

commit v4 on v3

--- a/solution.py
+++ b/solution.py
@@ -46,7 +46,7 @@
     maps, left, right, right3, rows, w_pair, w_proj, w_outp, update, partial, total, bias,
     q_buf, k_buf, v_buf, gate, done, w_out_v, w_project_v, w_output_v,
     left_s, left_r, right_s, right_r, rows_s, rows_r, sum_s, sum_r, bias_s, bias_r,
-    out_s, out_r, load_s,
+    out_s, out_r, own_s, load_s,
 ):
     seqs, res, cm = align_ref.shape
     row_block = pair_ref.shape[0]
@@ -114,8 +114,6 @@
 
         lax.fori_loop(1, n_res, send, 0)
 
-    pl.semaphore_wait(barrier, devices - 1)
-    send_rows(0)
     maps[:, : 2 * chan] = dot3(split(normed), split(w_in_ref[...]), ROWS_ROWS)
     source = lax.broadcasted_iota(jnp.int32, (2 * chan, 2 * width), 0)
     column = lax.broadcasted_iota(jnp.int32, (2 * chan, 2 * width), 1)
@@ -127,6 +125,7 @@
         placed = placed + (dot(high, pick) + dot(low, pick))
     left[chip] = placed[:, :width]
     right[core] = placed[:, width:]
+    pl.semaphore_wait(barrier, devices - 1)
 
     def left_copy(to, slot):
         return res_copy(
@@ -145,6 +144,7 @@
     right_copy(core).start()
     lax.fori_loop(1, chips, send_left, 0)
 
+    send_rows(0)
     send_rows(1)
     rows[:, pl.ds(pl.multiple_of(me * res, res), res), :] = align_ref[pl.ds(me * group, group)]
 
@@ -228,7 +228,6 @@
         lax.fori_loop(1, n_res, wait_rows, 0)
         lax.fori_loop(part * half, (part + 1) * half, project, 0)
 
-    project_part(0)
 
     partial[my_seq, core] = update[my_seq, core]
     for a in range(n_seq):
@@ -278,6 +277,7 @@
 
     lax.fori_loop(1, devices, send_bias, 0)
 
+    project_part(0)
     project_part(1)
 
     def wait_bias(t, c):
@@ -294,6 +294,12 @@
             done.at[s, pl.ds(pl.multiple_of(peer * res, res), res)],
             out_ref.at[slot * group + s],
             out_s.at[s, peer], out_r.at[s, slot], to,
+        )
+
+    def own_copy(s):
+        return pltpu.make_async_copy(
+            done.at[s, pl.ds(pl.multiple_of(me * res, res), res)],
+            out_ref.at[me * group + s], own_s.at[s],
         )
 
     def attend(s, c):
@@ -325,7 +331,7 @@
                 mixed.append(acc)
         gated = gate[s] * jnp.concatenate(mixed, axis=0)
         done[s] = rows[s] + dot3(split(gated), (w_outp[0], w_outp[1]))
-        out_ref[me * group + s] = done[s, pl.ds(pl.multiple_of(me * res, res), res), :]
+        own_copy(s).start()
 
         def send_out(t, d):
             peer = lax.rem(me + t, n_res)
@@ -350,6 +356,12 @@
         return c
 
     lax.fori_loop(1, n_res, finish, 0)
+
+    def finish_own(s, c):
+        own_copy(s).wait()
+        return c
+
+    lax.fori_loop(0, group, finish_own, 0)
 
     def finish_left(t, c):
         left_copy(lax.rem(chip + t, chips), chip).wait_send()
@@ -407,12 +419,13 @@
         pltpu.VMEM(w_output.shape, F32),
         dma((chips,)), dma((chips,)), dma((1,)), dma((1,)), dma((2, n_res)), dma((2, n_res)),
         dma((n_seq, PAIR)), dma((n_seq, PAIR)), dma((n_seq * n_res,)), dma((n_seq * n_res,)),
-        dma((group, n_res)), dma((group, n_res)), dma((3,)),
+        dma((group, n_res)), dma((group, n_res)), dma((group,)), dma((3,)),
     ]
     vectors = [a.reshape(1, -1) if a.ndim == 1 else a for a in args]
     vectors[3] = w_in.T
     vectors[6] = w_bias.T
-    hbm = pl.BlockSpec(memory_space=pl.ANY)
+    hbm = pl.BlockSpec(memory_space=pltpu.HBM)
+    free = pl.BlockSpec(memory_space=pl.ANY)
     return pl.pallas_call(
         functools.partial(kernel, n_seq, n_res, heads),
         out_shape=(
@@ -420,10 +433,10 @@
             jax.ShapeDtypeStruct(pair.shape, F32),
         ),
         in_specs=[hbm if k in (4, 8, 9) else vmem for k in range(len(args))],
-        out_specs=(vmem, vmem),
+        out_specs=(free, vmem),
         scratch_shapes=scratch,
         compiler_params=pltpu.CompilerParams(
-            collective_id=0, has_side_effects=True, vmem_limit_bytes=60 * 1024 * 1024
+            collective_id=0, has_side_effects=True, vmem_limit_bytes=24 * 1024 * 1024
         ),
     )(*vectors)
 

time: 56.4 us -> 55.4 us (0.982)
  Pallas kernels: 53 us -> 46.3 us
  local copies, waits for them, and re-layouts: 2.53 us -> 8.04 us
    pallas_call x1, Pallas kernels: 53 us -> 46.3 us  [on_device(): pl.pallas_call(functools.partial(kernel, n_seq, n_res, heads), out_shape=...]
    unnamed x4 -> x22, local copies, waits for them, and re-layouts: 2.53 us -> 8.04 us
where the time goes in v4:
time: 55.4 us; the launch traced here: 55 us
  Pallas kernels  46.3 us (84%)
  local copies, waits for them, and re-layouts  8.04 us (15%)
  between operations  0.68 us (1%)
    pallas_call x1, Pallas kernels, on_device(): pl.pallas_call(functools.partial(kernel, n_seq, n_res, heads), out_shape=...  46.3 us
    unnamed x22, local copies, waits for them, and re-layouts  8.04 us

profile of v4, /device:TPU:0, one launch (start us, length us, event | category | flops | bytes accessed | tf_op | source)
XLA Modules:
  0.0 55.0 jit_solution(3514984932270106191)
XLA Ops:
  0.6 0.0 copy-start.6
  0.6 0.0 copy-start.8
  0.7 0.0 copy-start.7
  0.7 0.0 copy-start.9
  0.7 0.6 %copy-done.6 = f32[128,8]{0,1:T(8,128)S(1)} copy-done((f32[128,8]{0,1:T(8,128)S(1)}, f32[128,8]{0,1:T(8,128)}, u32[]{:S(2)}) %copy-start.6) | copy-done | bytes 4120
  1.3 0.0 copy-done.8
  1.3 0.0 copy-done.7
  1.3 0.0 copy-done.9
  1.3 0.0 copy-start
  1.4 1.2 %copy-done = f32[256,1024]{1,0:T(8,128)S(1)} copy-done((f32[256,1024]{1,0:T(8,128)S(1)}, f32[256,1024]{1,0:T(8,128)}, u32[]{:S(2)}) %copy-start) | copy-done | bytes 1048600
  2.6 0.0 copy-start.1
  2.6 1.0 %copy-done.1 = f32[64,8,256]{2,1,0:T(8,128)S(1)} copy-done((f32[64,8,256]{2,1,0:T(8,128)S(1)}, f32[64,8,256]{2,1,0:T(8,128)}, u32[]{:S(2)}) %copy-start.1) | copy-done | bytes 524312
  3.6 0.0 copy-start.2
  3.6 1.0 %copy-done.2 = f32[1024,128]{1,0:T(8,128)S(1)} copy-done((f32[1024,128]{1,0:T(8,128)S(1)}, f32[1024,128]{1,0:T(8,128)}, u32[]{:S(2)}) %copy-start.2) | copy-done | bytes 524312
  4.7 0.0 copy-start.3
  4.7 0.9 %copy-done.3 = f32[256,256]{1,0:T(8,128)S(1)} copy-done((f32[256,256]{1,0:T(8,128)S(1)}, f32[256,256]{1,0:T(8,128)}, u32[]{:S(2)}) %copy-start.3) | copy-done | bytes 262168
  5.6 0.0 copy-start.4
  5.6 0.8 %copy-done.4 = f32[16,8,128]{2,1,0:T(8,128)S(1)} copy-done((f32[16,8,128]{2,1,0:T(8,128)S(1)}, f32[16,8,128]{2,1,0:T(8,128)}, u32[]{:S(2)}) %copy-start.4) | copy-done | bytes 65560
  6.4 0.0 copy-start.5
  6.5 0.8 %copy-done.5 = f32[256,64]{0,1:T(8,128)S(1)} copy-done((f32[256,64]{0,1:T(8,128)S(1)}, f32[256,64]{0,1:T(8,128)}, u32[]{:S(2)}) %copy-start.5) | copy-done | bytes 65560
  7.3 46.3 %shard_map.113 = (f32[64,8,256]{2,1,0:T(8,128)S(1)}, f32[16,8,128]{2,1,0:T(8,128)S(1)}) custom-call(f32[64,8,256]{2,1,0:T(8,128)S(1)} %copy-done.1, f32[16,8,128]{2,1,0:T(8,128)S(1)} %copy-done.4, f32[1,256]{1,0:T(1,128)S(1)} %bitcast.7, f32[64,256]{1,0:T(8,128)S(1)} %bitcast.5, f32[1024,128]{1,0:T(8,128)S(1)} %copy-done.2, f32[1,128]{1,0:T(1,128)S(1)} %bitcast.9, ...), custom_call_target="tpu_custom_call" | custom-call | tf_op jit(solution)/shard_map/pallas_call | solution.py:429
  53.6 0.8 %copy.14 = f32[64,8,256]{2,1,0:T(8,128)} copy(f32[64,8,256]{2,1,0:T(8,128)S(1)} %get-tuple-element.4) | data formatting | bytes 1048576
  54.4 0.6 %copy.15 = f32[16,8,128]{2,1,0:T(8,128)} copy(f32[16,8,128]{2,1,0:T(8,128)S(1)} %get-tuple-element.5) | data formatting | bytes 131072
Async XLA Ops:
  0.6 0.7 %copy-start.6 = (f32[128,8]{0,1:T(8,128)S(1)}, f32[128,8]{0,1:T(8,128)}, u32[]{:S(2)}) copy-start(f32[128,8]{0,1:T(8,128)} %param.16) | copy-start | bytes 12292
  0.6 0.7 %copy-start.8 = (f32[256]{0:T(256)S(1)}, f32[256]{0:T(256)}, u32[]{:S(2)}) copy-start(f32[256]{0:T(256)} %param.17) | copy-start | bytes 3076
  0.7 0.7 %copy-start.7 = (f32[256]{0:T(256)S(1)}, f32[256]{0:T(256)}, u32[]{:S(2)}) copy-start(f32[256]{0:T(256)} %param.12) | copy-start | bytes 3076
  0.7 0.7 %copy-start.9 = (f32[128]{0:T(128)S(1)}, f32[128]{0:T(128)}, u32[]{:S(2)}) copy-start(f32[128]{0:T(128)} %param.15) | copy-start | bytes 1540
  1.3 1.2 %copy-start = (f32[256,1024]{1,0:T(8,128)S(1)}, f32[256,1024]{1,0:T(8,128)}, u32[]{:S(2)}) copy-start(f32[256,1024]{1,0:T(8,128)} %w_project_ref.1) | copy-start | bytes 3145732
  2.6 1.0 %copy-start.1 = (f32[64,8,256]{2,1,0:T(8,128)S(1)}, f32[64,8,256]{2,1,0:T(8,128)}, u32[]{:S(2)}) copy-start(f32[64,8,256]{2,1,0:T(8,128)} %align_ref.1) | copy-start | bytes 1572868
  3.6 1.0 %copy-start.2 = (f32[1024,128]{1,0:T(8,128)S(1)}, f32[1024,128]{1,0:T(8,128)}, u32[]{:S(2)}) copy-start(f32[1024,128]{1,0:T(8,128)} %w_out_ref.1) | copy-start | bytes 1572868
  4.7 0.9 %copy-start.3 = (f32[256,256]{1,0:T(8,128)S(1)}, f32[256,256]{1,0:T(8,128)}, u32[]{:S(2)}) copy-start(f32[256,256]{1,0:T(8,128)} %w_output_ref.1) | copy-start | bytes 786436
  5.6 0.8 %copy-start.4 = (f32[16,8,128]{2,1,0:T(8,128)S(1)}, f32[16,8,128]{2,1,0:T(8,128)}, u32[]{:S(2)}) copy-start(f32[16,8,128]{2,1,0:T(8,128)} %pair_ref.1) | copy-start | bytes 196612
  6.4 0.8 %copy-start.5 = (f32[256,64]{0,1:T(8,128)S(1)}, f32[256,64]{0,1:T(8,128)}, u32[]{:S(2)}) copy-start(f32[256,64]{0,1:T(8,128)} %param.13) | copy-start | bytes 196612

commit v5 on v4

--- a/solution.py
+++ b/solution.py
@@ -226,7 +226,8 @@
             return c
 
         lax.fori_loop(1, n_res, wait_rows, 0)
-        lax.fori_loop(part * half, (part + 1) * half, project, 0)
+        for s in range(part * half, (part + 1) * half):
+            project(s, 0)
 
 
     partial[my_seq, core] = update[my_seq, core]
@@ -425,7 +426,6 @@
     vectors[3] = w_in.T
     vectors[6] = w_bias.T
     hbm = pl.BlockSpec(memory_space=pltpu.HBM)
-    free = pl.BlockSpec(memory_space=pl.ANY)
     return pl.pallas_call(
         functools.partial(kernel, n_seq, n_res, heads),
         out_shape=(
@@ -433,10 +433,10 @@
             jax.ShapeDtypeStruct(pair.shape, F32),
         ),
         in_specs=[hbm if k in (4, 8, 9) else vmem for k in range(len(args))],
-        out_specs=(free, vmem),
+        out_specs=(vmem, vmem),
         scratch_shapes=scratch,
         compiler_params=pltpu.CompilerParams(
-            collective_id=0, has_side_effects=True, vmem_limit_bytes=24 * 1024 * 1024
+            collective_id=0, has_side_effects=True, vmem_limit_bytes=60 * 1024 * 1024
         ),
     )(*vectors)
 

time: 55.4 us -> 51.5 us (0.930)
  local copies, waits for them, and re-layouts: 8.04 us -> 2.53 us
  Pallas kernels: 46.3 us -> 48.1 us
    unnamed x22 -> x4, local copies, waits for them, and re-layouts: 8.04 us -> 2.53 us
    pallas_call x1, Pallas kernels: 46.3 us -> 48.1 us  [on_device(): pl.pallas_call(functools.partial(kernel, n_seq, n_res, heads), out_shape=...]
where the time goes in v5:
time: 51.5 us; the launch traced here: 51.3 us
  Pallas kernels  48.1 us (93%)
  local copies, waits for them, and re-layouts  2.53 us (5%)
  between operations  0.65 us (1%)
    pallas_call x1, Pallas kernels, on_device(): pl.pallas_call(functools.partial(kernel, n_seq, n_res, heads), out_shape=...  48.1 us
    unnamed x4, local copies, waits for them, and re-layouts  2.53 us

profile of v5, /device:TPU:0, one launch (start us, length us, event | category | flops | bytes accessed | tf_op | source)
XLA Modules:
  0.0 51.3 jit_solution(97820295170773825)
XLA Ops:
  0.6 48.1 %shard_map.113 = (f32[64,8,256]{2,1,0:T(8,128)}, f32[16,8,128]{2,1,0:T(8,128)}) custom-call(f32[64,8,256]{2,1,0:T(8,128)} %align_ref.1, f32[16,8,128]{2,1,0:T(8,128)} %pair_ref.1, f32[1,256]{1,0:T(1,128)} %bitcast.7, f32[64,256]{1,0:T(8,128)} %bitcast.5, f32[1024,128]{1,0:T(8,128)} %w_out_ref.1, f32[1,128]{1,0:T(1,128)} %bitcast.9, f32[8,128]{1,0:T(8,128)} %bitcast.6, ...), custom_call_target="tpu_custom_call" | custom-call | tf_op jit(solution)/shard_map/pallas_call | solution.py:429
  48.8 0.0 copy-start
  48.8 1.9 %copy.14 = f32[64,8,256]{2,1,0:T(8,128)} copy(f32[64,8,256]{2,1,0:T(8,128)} %get-tuple-element.4) | data formatting | bytes 1048576
  50.7 0.0 copy-done
  50.7 0.6 %copy.15 = f32[16,8,128]{2,1,0:T(8,128)} copy(f32[16,8,128]{2,1,0:T(8,128)S(1)} %copy-done) | data formatting | bytes 131072
Async XLA Ops:
  48.8 1.9 %copy-start = (f32[16,8,128]{2,1,0:T(8,128)S(1)}, f32[16,8,128]{2,1,0:T(8,128)}, u32[]{:S(2)}) copy-start(f32[16,8,128]{2,1,0:T(8,128)} %get-tuple-element.5) | copy-start | bytes 196612
